TPU v7x, 32 devices: a whole 2x2x4 slice. The times are simulated.
32 devices in a mesh: section: 2 (over core), row: 4 (over y, x), col: 4 (over z).
Axes of the slice: x: 2, y: 2, z: 4, core: 2. Of those that a mesh axis runs over, the one named last changes fastest.
Arguments:
- out_grad: bfloat16 [2048, 256], P(('row', 'col')), may hold values from -6 to 6
- pre_act: bfloat16 [2, 2048, 256], P('section', ('row', 'col')), may hold values from -6 to 6
- aggregated: bfloat16 [2, 2048, 256], P('section', ('row', 'col')), may hold values from -6 to 6
- weights: bfloat16 [2, 256, 256], P('section'), may hold values from -0.375 to 0.375
- tiles: bfloat16 [4, 4, 64, 128, 128], P('row', 'col'), may hold values from -0.109375 to 0.109375
- tile_index: int32 [4, 4, 64, 2], P('row', 'col'), may hold values from 0 to 3, as said below
- live_count: int32 [4, 4], P('row', 'col'), may hold values from 8 to 64, as said below
Outputs:
- weight_grad: float32 [2, 256, 256], P('section')
- feature_grads: bfloat16 [2, 2048, 256], P('section', ('row', 'col'))
Inputs may be any that keep to these rules, and one draw needn't show every extreme that they name: `tile_index`: both entries index blocks of the tile: the first is under 4, the second under 4. `live_count`: some tile uses all 64 slots.
All inputs are finite; a program needn't handle non-finite values.
Results may differ from a plain program's by a relative error of at most 0.012.
Values may be sent and summed in bfloat16 or wider, within the bound.
A program may use at most 64 MiB of HBM per device.

v0:
```python
import math

import jax
import jax.numpy as jnp
from jax import lax
from jax.sharding import PartitionSpec as P


def from_behind(value, axis, steps):
    count = lax.axis_size(axis)
    leading, last = (max(0, -steps), min(count, count - steps))
    return lax.ppermute(value, axis, [(source, source + steps) for source in range(leading, last)])


def on_device(out_grad, pre_act, aggregated, weights, tiles, tile_index, live_count):
    section_id = lax.axis_index("section")
    upper = section_id == 1
    pre_layer = pre_act[0]
    saved_agg = aggregated[0]
    weight_mat = weights[0]
    tile_blocks = tiles[0, 0]
    tile_slots = tile_index[0, 0]
    tile_count = live_count[0, 0]
    node_rows = out_grad.shape[0]
    width = out_grad.shape[1]
    slot_total = tile_blocks.shape[0]
    block = tile_blocks.shape[1]
    tile_rows = node_rows * lax.axis_size("col")
    row_blocks = tile_rows // block
    group = min(32, slot_total)
    groups = slot_total // group
    grouped_slots = tile_slots.reshape(groups, group, 2)
    all_targets = jnp.arange(row_blocks, dtype=jnp.int32)

    def spread(row_grad):
        return lax.all_gather(row_grad, "row", axis=0, tiled=True)

    def block_total(source, col_blocks):
        height = source.shape[1]
        grouped_blocks = source.reshape(groups, group, height, block)

        def group_term(total, blocks_here, slots_here, first_slot):
            picked = jnp.take(col_blocks, slots_here[:, 1], axis=0)
            products = jnp.einsum(
                "sij,sjf->sif", blocks_here, picked, preferred_element_type=jnp.float32
            )
            slot_ids = first_slot + jnp.arange(group, dtype=jnp.int32)
            live = slot_ids < tile_count
            select = ((slots_here[:, 0][None, :] == all_targets[:, None]) & live[None, :]).astype(
                jnp.float32
            )
            return total + jnp.einsum("bs,sif->bif", select, products)

        start_total = jnp.zeros((row_blocks, height, width), jnp.float32)

        def scan_step(total, group_id):
            blocks_here = lax.dynamic_index_in_dim(grouped_blocks, group_id, 0, False)
            slots_here = lax.dynamic_index_in_dim(grouped_slots, group_id, 0, False)
            return (group_term(total, blocks_here, slots_here, group_id * group), None)

        total, _ = lax.scan(scan_step, start_total, jnp.arange(groups, dtype=jnp.int32))
        return total.reshape(row_blocks * height, width)

    def reduce_col(source, gathered):
        col_blocks = gathered.reshape(-1, block, width)
        height = source.shape[1]
        return lax.psum_scatter(
            block_total(source, col_blocks), "col", scatter_dimension=0, tiled=True
        )

    def local_terms(incoming):
        masked = jnp.where(pre_layer > 0, incoming, jnp.zeros_like(incoming))
        weight_term = lax.dot_general(
            saved_agg, masked, (((0,), (0,)), ((), ())), preferred_element_type=jnp.float32
        )
        row_grad = lax.dot_general(
            masked, weight_mat, (((1,), (1,)), ((), ())), preferred_element_type=jnp.float32
        ).astype(jnp.bfloat16)
        return (weight_term, row_grad)

    def backward_step(incoming):
        weight_term, row_grad = local_terms(incoming)
        summed = reduce_col(tile_blocks, spread(row_grad))
        return (weight_term, summed.astype(jnp.bfloat16))

    first_input = jnp.where(upper, out_grad, jnp.zeros_like(out_grad))
    first_weight, first_grad = backward_step(first_input)
    received = from_behind(first_grad, "section", -1)
    second_weight, second_grad = backward_step(received)
    local_weight = jnp.where(upper, first_weight, second_weight)
    feature_block = jnp.where(upper, first_grad, second_grad)
    total_weight = lax.psum(local_weight, ("row", "col"))
    node_total = node_rows * lax.axis_size("row") * lax.axis_size("col")
    weight_grad = (total_weight * (1.0 / math.sqrt(node_total)))[None]
    return (weight_grad, feature_block[None])


def solution(mesh):
    placed = (
        P(("row", "col"), None),
        P("section", ("row", "col"), None),
        P("section", ("row", "col"), None),
        P("section", None, None),
        P("row", "col", None, None, None),
        P("row", "col", None, None),
        P("row", "col"),
    )
    return jax.shard_map(
        on_device,
        mesh=mesh,
        in_specs=placed,
        out_specs=(P("section", None, None), P("section", ("row", "col"), None)),
        check_vma=False,
    )
```

profile of v0, /device:TPU:0, one launch (start us, length us, event | category | flops | bytes accessed | tf_op | source)
XLA Modules:
  0.0 212.3 jit_solution(15838875846190478118)
XLA Ops:
  7.2 0.0 copy-start
  7.2 0.0 reduce-scatter.3.cloned.1.call-start
  7.2 0.9 broadcast_compare_fusion
  8.1 0.2 convolution_convert_fusion.1
  8.3 10.5 %all_gather.6 = bf16[512,256]{1,0:T(8,128)(2,1)S(1)} all-gather(bf16[128,256]{1,0:T(8,128)(2,1)S(1)} %convolution_convert_fusion.1), channel_id=1, replica_groups=mesh['section'=2,'row'=4,'col'=4] {'row'}, dimensions={0}, use_global_device_ids=true | all-gather | bytes 327680 | tf_op jit(solution)/shard_map/all_gather | solution.py:36
  18.8 0.8 reshape_squeeze.7
  19.6 20.1 %while.22 = (s32[]{:T(128)}, f32[4,128,256]{2,0,1:T(4,128)S(1)}, s32[2]{0:T(128)S(1)}, s32[2,32,2]{1,2,0:T(2,128)S(1)}, s32[]{:T(128)}, /*index=5*/bf16[2,32,128...) while((s32[]{:T(128)}, f32[4,128,256]{2,0,1:T(4,128)S(1)}, ...), condition=%wide.region_1.3_spmd.clone, body=%wide.region_0.2_spmd.clone.sunk | while | flops 278136320 | bytes 12588737 | solution.py:61
  19.6 0.6 dynamic_slice.45
  22.2 2.0 gather_fusion
  24.2 2.7 %fusion.70 = bf16[32,128,256]{2,1,0:T(8,128)(2,1)S(1)} fusion(bf16[32,128,256]{2,1,0:T(8,128)(2,1)} %gather_fusion, pred[32]{0:T(512)(128)(4,1)S(1)} %get-tuple-element.273, bf16[2,32,128,128]{3,2,1,0:T(8,128)(2,1)} %get-tuple-element.310, s32[]{:T(128)S(6)} %select_n.94), kind=kOutput, calls=%fused_computation.6.clone.1 | convolution fusion | flops 269484032 | bytes 5242916 | tf_op jit(solution)/shard_map/while/body/eval_jaxpr/sij,sjf->sif/dot_general | solution.py:44
  27.6 0.7 add_compare_fusion.4
  28.2 1.4 fusion.71
  29.7 0.6 dynamic_slice.45
  32.3 2.0 gather_fusion
  34.3 2.7 %fusion.70 = bf16[32,128,256]{2,1,0:T(8,128)(2,1)S(1)} fusion(bf16[32,128,256]{2,1,0:T(8,128)(2,1)} %gather_fusion, pred[32]{0:T(512)(128)(4,1)S(1)} %get-tuple-element.273, bf16[2,32,128,128]{3,2,1,0:T(8,128)(2,1)} %get-tuple-element.310, s32[]{:T(128)S(6)} %select_n.94), kind=kOutput, calls=%fused_computation.6.clone.1 | convolution fusion | flops 269484032 | bytes 5242916 | tf_op jit(solution)/shard_map/while/body/eval_jaxpr/sij,sjf->sif/dot_general | solution.py:44
  37.6 0.7 add_compare_fusion.4
  38.3 1.4 fusion.71
  39.7 0.9 copy.10
  40.6 0.0 reduce-scatter.3.cloned.1.call-update
  40.7 0.0 all-reduce.2.cloned.1.call-start
  40.7 22.0 %reduce-scatter.3.cloned.1.call-done = f32[128,256]{1,0:T(8,128)} async-done(((f32[512,256]{1,0:T(8,128)}), f32[128,256]{1,0:T(8,128)}) %reduce-scatter.3.cloned.1.call-update) | async-done | bytes 131088 | tf_op jit(solution)/shard_map/reduce_scatter | solution.py:67
  62.7 0.9 convert_element_type.15
  63.7 1.3 collective-permute-start
  65.0 0.2 fusion.44
  65.2 1.6 collective-permute-done
  66.8 0.2 convolution_convert_fusion
  67.0 8.9 %all_gather.7 = bf16[512,256]{1,0:T(8,128)(2,1)S(1)} all-gather(bf16[128,256]{1,0:T(8,128)(2,1)S(1)} %convolution_convert_fusion), channel_id=1, replica_groups=mesh['section'=2,'row'=4,'col'=4] {'row'}, dimensions={0}, use_global_device_ids=true | all-gather | bytes 327680 | tf_op jit(solution)/shard_map/all_gather | solution.py:36
  75.9 0.9 fusion.40
  76.9 0.0 all-reduce.2.cloned.1.call-update
  76.9 0.0 reduce-scatter.5.cloned.1.call-start
  77.0 19.5 %while.23 = (s32[]{:T(128)}, f32[4,128,256]{2,0,1:T(4,128)S(1)}, s32[2]{0:T(128)S(1)}, s32[2,32,2]{1,2,0:T(2,128)S(1)}, s32[]{:T(128)}, /*index=5*/bf16[2,32,128...) while((s32[]{:T(128)}, f32[4,128,256]{2,0,1:T(4,128)S(1)}, ...), condition=%wide.region_5.7_spmd.clone, body=%wide.region_4.6_spmd.clone.sunk | while | flops 278136320 | bytes 12588737 | solution.py:61
  77.0 0.6 dynamic_slice.48
  79.3 2.0 gather_fusion.1
  81.3 2.7 %fusion.76 = bf16[32,128,256]{2,1,0:T(8,128)(2,1)S(1)} fusion(bf16[32,128,256]{2,1,0:T(8,128)(2,1)} %gather_fusion.1, pred[32]{0:T(512)(128)(4,1)S(1)} %get-tuple-element.282, bf16[2,32,128,128]{3,2,1,0:T(8,128)(2,1)} %get-tuple-element.343, s32[]{:T(128)S(6)} %select_n.96), kind=kOutput, calls=%fused_computation.28.clone.1 | convolution fusion | flops 269484032 | bytes 5242916 | tf_op jit(solution)/shard_map/while/body/eval_jaxpr/sij,sjf->sif/dot_general | solution.py:44
  84.6 0.7 add_compare_fusion.5
  85.2 1.4 fusion.77
  86.7 0.6 dynamic_slice.48
  89.0 2.0 gather_fusion.1
  91.0 2.7 %fusion.76 = bf16[32,128,256]{2,1,0:T(8,128)(2,1)S(1)} fusion(bf16[32,128,256]{2,1,0:T(8,128)(2,1)} %gather_fusion.1, pred[32]{0:T(512)(128)(4,1)S(1)} %get-tuple-element.282, bf16[2,32,128,128]{3,2,1,0:T(8,128)(2,1)} %get-tuple-element.343, s32[]{:T(128)S(6)} %select_n.96), kind=kOutput, calls=%fused_computation.28.clone.1 | convolution fusion | flops 269484032 | bytes 5242916 | tf_op jit(solution)/shard_map/while/body/eval_jaxpr/sij,sjf->sif/dot_general | solution.py:44
  94.3 0.7 add_compare_fusion.5
  95.0 1.4 fusion.77
  96.4 0.9 copy.12
  97.3 0.0 reduce-scatter.5.cloned.1.call-update
  97.3 83.9 %all-reduce.2.cloned.1.call-done = f32[256,256]{0,1:T(8,128)} async-done(((f32[256,256]{0,1:T(8,128)}), f32[256,256]{0,1:T(8,128)}) %all-reduce.2.cloned.1.call-update) | async-done | bytes 262160 | tf_op jit(solution)/shard_map/psum | solution.py:92
  181.2 1.0 multiply_bitcast_fusion
  182.2 0.8 copy.13
  183.0 21.3 %reduce-scatter.5.cloned.1.call-done = f32[128,256]{1,0:T(8,128)} async-done(((f32[512,256]{1,0:T(8,128)}), f32[128,256]{1,0:T(8,128)}) %reduce-scatter.5.cloned.1.call-update) | async-done | bytes 131088 | tf_op jit(solution)/shard_map/reduce_scatter | solution.py:67
  204.3 1.5 select_bitcast_fusion
  (28 shorter events, 0.1 us)
Async XLA Ops:
  7.2 0.9 copy-start
  7.2 55.6 %reduce-scatter.3.cloned.1.call-start = ((), (), s32[]{:S(2)}) async-start(), calls=%async_computation.2 | async-start | bytes 655360 | tf_op jit(solution)/shard_map/reduce_scatter | solution.py:67
  19.6 45.4 %copy-start.2 = (bf16[1,128,256]{2,1,0:T(8,128)(2,1)S(1)}, bf16[1,128,256]{2,1,0:T(8,128)(2,1)}, u32[]{:S(2)}) copy-start(bf16[1,128,256]{2,1,0:T(8,128)(2,1)} %param.15) | copy-start | bytes 196612
  19.6 45.4 %copy-start.3 = (bf16[128,256]{1,0:T(8,128)(2,1)S(1)}, bf16[128,256]{1,0:T(8,128)(2,1)}, u32[]{:S(2)}) copy-start(bf16[128,256]{1,0:T(8,128)(2,1)} %param.13) | copy-start | bytes 196612
  40.7 140.5 %all-reduce.2.cloned.1.call-start = ((), (), s32[]{:S(2)}) async-start(), calls=%async_computation.3 | async-start | bytes 524288 | tf_op jit(solution)/shard_map/psum | solution.py:92
  63.7 3.1 %collective-permute-start = (bf16[128,256]{1,0:T(8,128)(2,1)S(1)}, bf16[128,256]{1,0:T(8,128)(2,1)S(1)}, u32[]{:S(2)}, u32[]{:S(2)}) collective-permute-start(bf16[128,256]{1,0:T(8,128)(2,1)S(1)} %convert_element_type.15), channel_id=1, source_target_pairs={{16,0},{17,1},{18,2},{19,3},{20,4},{21,5},{22,6},{23,7},{24,8},{25... | collective-permute-start | bytes 196616 | tf_op jit(solution)/shard_map/ppermute | solution.py:12
  76.9 127.4 %reduce-scatter.5.cloned.1.call-start = ((), (), s32[]{:S(2)}) async-start(), calls=%async_computation.4 | async-start | bytes 655360 | tf_op jit(solution)/shard_map/reduce_scatter | solution.py:67
  96.4 107.9 %copy-start.1 = (f32[128,256]{1,0:T(8,128)S(1)}, f32[128,256]{1,0:T(8,128)}, u32[]{:S(2)}) copy-start(f32[128,256]{1,0:T(8,128)} %reduce-scatter.3.cloned.1.call-done) | copy-start | bytes 393220
Sparse Core Ops, SparseCore 0:
  40.8 21.9 reduce-scatter.2
  77.0 104.1 all-reduce.1
  183.6 20.6 reduce-scatter.4
where the time goes:
time: 213 us; the launch traced here: 212 us
  waiting for transfers between devices  129 us (61%)
  blocking collectives  19.4 us (9%)
  matrix products  18.1 us (8%)
  local copies, waits for them, and re-layouts  13.9 us (7%)
  between operations  13.9 us (7%)
  loops' own time  9.92 us (5%)
  other arithmetic  6.98 us (3%)
    psum x1, waiting for transfers between devices, on_device(): total_weight = lax.psum(local_weight, ('row', 'col'))  83.9 us
    reduce_scatter x2, waiting for transfers between devices, reduce_col(): lax.psum_scatter(block_total(source, col_blocks), 'col', scatter_dimensio...  43.3 us
    all_gather x2, blocking collectives, spread(): return lax.all_gather(row_grad, 'row', axis=0, tiled=True)  19.4 us
    dot_general x4, matrix products, group_term(): jnp.einsum('sij,sjf->sif', blocks_here, picked, preferred_element_type=jn...  10.8 us
    another operation x2, loops' own time, block_total(): lax.scan(scan_step, start_total, jnp.arange(groups, dtype=jnp.int32))  9.92 us
    gather x4, local copies, waits for them, and re-layouts, group_term(): picked = jnp.take(col_blocks, slots_here[:, 1], axis=0)  8.08 us
    dot_general x4, matrix products, group_term(): return total + jnp.einsum('bs,sif->bif', select, products)  5.75 us
  transfers between devices with their start and end apart: 4, of which 4 were waited for; matrix products, arithmetic and copies ran while one was open for 8% of the time, Pallas kernels for 0%

commit v1 on v0

--- a/solution.py
+++ b/solution.py
@@ -1,9 +1,210 @@
+import functools
 import math
 
 import jax
 import jax.numpy as jnp
 from jax import lax
+from jax.experimental import pallas as pl
+from jax.experimental.pallas import tpu as pltpu
 from jax.sharding import PartitionSpec as P
+
+MESH = pl.DeviceIdType.MESH
+CHUNKS = 4
+
+
+def dense_kernel(col_blocks, slots, count, tiles, dense, held, total, sems):
+    slot_total, block = held.shape[:2]
+    per = slot_total // CHUNKS
+
+    def fetch(part):
+        rows = pl.ds(part * per, per)
+        return pltpu.make_async_copy(tiles.at[rows], held.at[rows], sems.at[part])
+
+    for part in range(CHUNKS):
+        fetch(part).start()
+    total[...] = jnp.zeros_like(total)
+    live = count[0, 0]
+
+    def add(slot, carry):
+        place = slots[0, slot] * col_blocks + slots[1, slot]
+        total[place] += held[slot].astype(jnp.float32)
+        return carry
+
+    for part in range(CHUNKS):
+        fetch(part).wait()
+        lax.fori_loop(part * per, jnp.minimum(live, (part + 1) * per), add, 0)
+    for place in range(total.shape[0]):
+        r, c = divmod(place, col_blocks)
+        dense[pl.ds(r * block, block), pl.ds(c * block, block)] = total[place].astype(jnp.bfloat16)
+
+
+def layers_kernel(
+    R, C, scale, out_grad, pre, agg, weight, dense, wsum, feat,
+    inc, gath, part, got, wire, wgot, wfull,
+    row_send, row_recv, col_send, col_recv, ws_send, ws_recv, wg_send, wg_recv, hand_send, hand_recv,
+):
+    sec, r, c = (lax.axis_index(a) for a in ("section", "row", "col"))
+    N = R * C
+    me = r * C + c
+    nodes, width = out_grad.shape
+    chunk = wire.shape[1]
+
+    def peer(p):
+        return (sec, p // C, lax.rem(p, C))
+
+    barrier = pltpu.get_barrier_semaphore()
+    for d in range(1, N):
+        pl.semaphore_signal(barrier, inc=1, device_id=peer(lax.rem(me + d, N)), device_id_type=MESH)
+    pl.semaphore_signal(barrier, inc=1, device_id=(1 - sec, r, c), device_id_type=MESH)
+
+    def copy(src, dst, send, recv, to):
+        return pltpu.make_async_remote_copy(
+            src_ref=src, dst_ref=dst, send_sem=send, recv_sem=recv, device_id=to, device_id_type=MESH
+        )
+
+    def row_copy(d, slot):
+        return copy(gath.at[slot], gath.at[slot], row_send.at[d - 1], row_recv.at[d - 1], (sec, lax.rem(r + d, R), c))
+
+    def col_copy(d, slot):
+        to = lax.rem(c + d, C)
+        return copy(part.at[d - 1], got.at[d - 1], col_send.at[d - 1], col_recv.at[d - 1], (sec, r, to))
+
+    def ws_copy(d):
+        to = lax.rem(me + d, N)
+        return copy(wire.at[to], wgot.at[d - 1], ws_send.at[d - 1], ws_recv.at[d - 1], peer(to))
+
+    def wg_copy(d, slot):
+        return copy(wfull.at[slot], wfull.at[slot], wg_send.at[d - 1], wg_recv.at[d - 1], peer(lax.rem(me + d, N)))
+
+    def hand_copy():
+        return copy(feat, inc, hand_send, hand_recv, (1 - sec, r, c))
+
+    @pl.when(sec == 1)
+    def _():
+        inc[...] = out_grad[...]
+
+    pl.semaphore_wait(barrier, N)
+
+    @pl.when(sec == 0)
+    def _():
+        hand_copy().wait_recv()
+
+    masked = jnp.where(pre[...] > 0, inc[...], jnp.zeros((nodes, width), jnp.bfloat16))
+    gath[r] = lax.dot_general(
+        masked, weight[...], (((1,), (1,)), ((), ())), preferred_element_type=jnp.float32
+    ).astype(jnp.bfloat16)
+    for d in range(1, R):
+        row_copy(d, r).start()
+
+    wire[...] = lax.dot_general(
+        agg[...], masked, (((0,), (0,)), ((), ())), preferred_element_type=jnp.float32
+    ).astype(jnp.bfloat16).reshape(wire.shape)
+
+    def start_weight():
+        for d in range(1, N):
+            ws_copy(d).start()
+
+    def gather_weight():
+        total = wire[me].astype(jnp.float32)
+        for d in range(1, N):
+            ws_copy(d).wait_recv()
+            total = total + wgot[d - 1].astype(jnp.float32)
+        wfull[me] = (total * scale).astype(jnp.bfloat16)
+        for d in range(1, N):
+            wg_copy(d, me).start()
+
+    @pl.when(sec == 0)
+    def _():
+        start_weight()
+
+    for d in range(1, R):
+        row_copy(d, lax.rem(r + R - d, R)).wait_recv()
+    spread = gath[...].reshape(R * nodes, width)
+
+    def term(to):
+        rows = pl.ds(pl.multiple_of(to * nodes, nodes), nodes)
+        return jnp.dot(dense[rows, :], spread, preferred_element_type=jnp.float32)
+
+    for d in range(1, C):
+        part[d - 1] = term(lax.rem(c + d, C)).astype(jnp.bfloat16)
+        col_copy(d, c).start()
+    total = term(c)
+
+    @pl.when(sec == 0)
+    def _():
+        gather_weight()
+
+    for d in range(1, C):
+        col_copy(d, c).wait_recv()
+        total = total + got[d - 1].astype(jnp.float32)
+    feat[...] = total.astype(jnp.bfloat16)
+
+    @pl.when(sec == 1)
+    def _():
+        hand_copy().start()
+        start_weight()
+        gather_weight()
+        hand_copy().wait_send()
+
+    for d in range(1, N):
+        wg_copy(d, lax.rem(me + N - d, N)).wait_recv()
+    wsum[...] = wfull[...]
+    for d in range(1, R):
+        row_copy(d, r).wait_send()
+    for d in range(1, C):
+        col_copy(d, c).wait_send()
+    for d in range(1, N):
+        ws_copy(d).wait_send()
+        wg_copy(d, me).wait_send()
+
+
+def fused(out_grad, pre_act, aggregated, weights, tiles, tile_index, live_count):
+    R, C = lax.axis_size("row"), lax.axis_size("col")
+    N = R * C
+    nodes, width = out_grad.shape
+    slot_total, block = tiles.shape[2:4]
+    rows, cols = C * nodes, R * nodes
+    row_blocks, col_blocks = rows // block, cols // block
+    vmem = pl.BlockSpec(memory_space=pltpu.VMEM)
+    smem = pl.BlockSpec(memory_space=pltpu.SMEM)
+    bf16, f32, dma = jnp.bfloat16, jnp.float32, pltpu.SemaphoreType.DMA
+    dense = pl.pallas_call(
+        functools.partial(dense_kernel, col_blocks),
+        out_shape=jax.ShapeDtypeStruct((rows, cols), bf16),
+        in_specs=[smem, smem, pl.BlockSpec(memory_space=pl.ANY)],
+        out_specs=vmem,
+        scratch_shapes=[
+            pltpu.VMEM((slot_total, block, block), bf16),
+            pltpu.VMEM((row_blocks * col_blocks, block, block), f32),
+            dma((CHUNKS,)),
+        ],
+        name="dense_tile",
+    )(tile_index[0, 0].T, live_count, tiles[0, 0])
+    chunk = width // N
+    scale = 1.0 / math.sqrt(nodes * N)
+    wsum, feat = pl.pallas_call(
+        functools.partial(layers_kernel, R, C, scale),
+        out_shape=(
+            jax.ShapeDtypeStruct((N, chunk, width), bf16),
+            jax.ShapeDtypeStruct((nodes, width), bf16),
+        ),
+        in_specs=[vmem] * 5,
+        out_specs=(vmem, vmem),
+        scratch_shapes=[
+            pltpu.VMEM((nodes, width), bf16),
+            pltpu.VMEM((R, nodes, width), bf16),
+            pltpu.VMEM((C - 1, nodes, width), bf16),
+            pltpu.VMEM((C - 1, nodes, width), bf16),
+            pltpu.VMEM((N, chunk, width), bf16),
+            pltpu.VMEM((N - 1, chunk, width), bf16),
+            pltpu.VMEM((N, chunk, width), bf16),
+            dma((R - 1,)), dma((R - 1,)), dma((C - 1,)), dma((C - 1,)),
+            dma((N - 1,)), dma((N - 1,)), dma((N - 1,)), dma((N - 1,)), dma, dma,
+        ],
+        compiler_params=pltpu.CompilerParams(collective_id=0, has_side_effects=True),
+        name="both_layers",
+    )(out_grad, pre_act[0], aggregated[0], weights[0], dense)
+    return (wsum.astype(f32).reshape(1, width, width), feat[None])
 
 
 def from_behind(value, axis, steps):
@@ -13,6 +214,11 @@
 
 
 def on_device(out_grad, pre_act, aggregated, weights, tiles, tile_index, live_count):
+    nodes, width = out_grad.shape
+    devices = lax.axis_size("row") * lax.axis_size("col")
+    dense_blocks = devices * (nodes // tiles.shape[3]) ** 2
+    if dense_blocks <= tiles.shape[2] and width % (16 * devices) == 0:
+        return fused(out_grad, pre_act, aggregated, weights, tiles, tile_index, live_count)
     section_id = lax.axis_index("section")
     upper = section_id == 1
     pre_layer = pre_act[0]

time: 213 us -> 37.9 us (0.18)
  waiting for transfers between devices: 129 us -> 0 us
  Pallas kernels: 0 us -> 33.3 us
  blocking collectives: 19.4 us -> 0 us
  matrix products: 18.1 us -> 0 us
  between operations: 13.9 us -> 1.29 us
  local copies, waits for them, and re-layouts: 13.9 us -> 1.47 us
  loops' own time: 9.92 us -> 0 us
  other arithmetic: 6.98 us -> 1.63 us
    psum x1 -> x0, waiting for transfers between devices: 83.9 us -> none  [on_device(): total_weight = lax.psum(local_weight, ('row', 'col'))]
    reduce_scatter x2 -> x0, waiting for transfers between devices: 43.3 us -> none  [reduce_col(): lax.psum_scatter(block_total(source, col_blocks), 'col', scatter_dimensio...]
    pallas_call x0 -> x2, Pallas kernels: none -> 33.3 us  [the longest x1 30.2 us: fused(): pl.pallas_call(functools.partial(layers_kernel, R, C, scale), out_shape=(...]
    all_gather x2 -> x0, blocking collectives: 19.4 us -> none  [spread(): return lax.all_gather(row_grad, 'row', axis=0, tiled=True)]
    dot_general x12 -> x0, matrix products: 18.1 us -> none  [the longest x4 10.8 us: group_term(): jnp.einsum('sij,sjf->sif', blocks_here, picked, preferred_element_type=jn...]
    another operation x2 -> x0, loops' own time: 9.92 us -> none  [block_total(): lax.scan(scan_step, start_total, jnp.arange(groups, dtype=jnp.int32))]
    gather x4 -> x0, local copies, waits for them, and re-layouts: 8.08 us -> none  [group_term(): picked = jnp.take(col_blocks, slots_here[:, 1], axis=0)]
    lt x4 -> x0, other arithmetic: 2.61 us -> none  [group_term(): live = slot_ids < tile_count]
  transfers between devices with their start and end apart: 4 -> 0, of which waited for: 4 -> 0; matrix products, arithmetic and copies ran while one was open for 8% -> 0% of each run, Pallas kernels for 0% -> 0%
where the time goes in v1:
time: 37.9 us; the launch traced here: 37.7 us
  Pallas kernels  33.3 us (88%)
  other arithmetic  1.63 us (4%)
  local copies, waits for them, and re-layouts  1.47 us (4%)
  between operations  1.29 us (3%)
    pallas_call x1, Pallas kernels, fused(): pl.pallas_call(functools.partial(layers_kernel, R, C, scale), out_shape=(...  30.2 us
    pallas_call x1, Pallas kernels, fused(): pl.pallas_call(functools.partial(dense_kernel, col_blocks), out_shape=jax...  3.09 us
    reshape x1, other arithmetic, fused(): return (wsum.astype(f32).reshape(1, width, width), feat[None])  1.63 us
    unnamed x1, local copies, waits for them, and re-layouts  1.47 us

profile of v1, /device:TPU:0, one launch (start us, length us, event | category | flops | bytes accessed | tf_op | source)
XLA Modules:
  0.0 37.7 jit_solution(11606714565648740887)
XLA Ops:
  1.3 3.1 %dense_tile.1.dense = bf16[512,512]{1,0:T(8,128)(2,1)} custom-call(s32[2,64]{1,0:T(2,128)} %bitcast.18, s32[1,1]{1,0:T(1,128)S(6)} %copy.10.count, bf16[64,128,128]{2,1,0:T(8,128)(2,1)} %bitcast.12), custom_call_target="tpu_custom_call" | custom-call | tf_op jit(solution)/shard_map/dense_tile/pallas_call | solution.py:171
  4.4 30.2 %both_layers.1 = (bf16[16,16,256]{2,1,0:T(8,128)(2,1)}, bf16[128,256]{1,0:T(8,128)(2,1)}) custom-call(bf16[128,256]{1,0:T(8,128)(2,1)} %out_grad.1, bf16[128,256]{1,0:T(8,128)(2,1)} %bitcast.16, bf16[128,256]{1,0:T(8,128)(2,1)} %bitcast.17, bf16[256,256]{1,0:T(8,128)(2,1)} %bitcast.14, bf16[512,512]{1,0:T(8,128)(2,1)} %dense_tile.1.dense), custom_call_target="tpu_custom_call" | custom-call | tf_op jit(solution)/shard_map/both_layers/pallas_call | solution.py:185
  34.6 1.6 %bitcast_convert_fusion = f32[1,256,256]{2,1,0:T(8,128)} fusion(bf16[1,256,256]{2,1,0:T(8,128)(2,1)} %bitcast.13), kind=kLoop, calls=%fused_computation | loop fusion | flops 65536 | bytes 393216 | tf_op jit(solution)/shard_map/reshape | solution.py:207
  36.2 1.5 %copy.11 = bf16[1,128,256]{2,1,0:T(8,128)(2,1)} copy(bf16[1,128,256]{2,1,0:T(8,128)(2,1)} %bitcast.15) | data formatting | bytes 131072

commit v2 on v1

--- a/solution.py
+++ b/solution.py
@@ -40,22 +40,24 @@
 
 def layers_kernel(
     R, C, scale, out_grad, pre, agg, weight, dense, wsum, feat,
-    inc, gath, part, got, wire, wgot, wfull,
-    row_send, row_recv, col_send, col_recv, ws_send, ws_recv, wg_send, wg_recv, hand_send, hand_recv,
+    inc, gath, part, got, wire, xgot, along, summed,
+    row_send, row_recv, col_send, col_recv, hand_send, hand_recv,
+    wx_send, wx_recv, wz_send, wz_recv, wg_send, wg_recv,
 ):
     sec, r, c = (lax.axis_index(a) for a in ("section", "row", "col"))
-    N = R * C
-    me = r * C + c
     nodes, width = out_grad.shape
-    chunk = wire.shape[1]
-
-    def peer(p):
-        return (sec, p // C, lax.rem(p, C))
-
+
+    def row_peer(d):
+        return (sec, lax.rem(r + d, R), c)
+
+    def col_peer(d):
+        return (sec, r, lax.rem(c + d, C))
+
+    across = (1 - sec, r, c)
     barrier = pltpu.get_barrier_semaphore()
-    for d in range(1, N):
-        pl.semaphore_signal(barrier, inc=1, device_id=peer(lax.rem(me + d, N)), device_id_type=MESH)
-    pl.semaphore_signal(barrier, inc=1, device_id=(1 - sec, r, c), device_id_type=MESH)
+    peers = [row_peer(d) for d in range(1, R)] + [col_peer(d) for d in range(1, C)] + [across]
+    for to in peers:
+        pl.semaphore_signal(barrier, inc=1, device_id=to, device_id_type=MESH)
 
     def copy(src, dst, send, recv, to):
         return pltpu.make_async_remote_copy(
@@ -63,59 +65,51 @@
         )
 
     def row_copy(d, slot):
-        return copy(gath.at[slot], gath.at[slot], row_send.at[d - 1], row_recv.at[d - 1], (sec, lax.rem(r + d, R), c))
-
-    def col_copy(d, slot):
-        to = lax.rem(c + d, C)
-        return copy(part.at[d - 1], got.at[d - 1], col_send.at[d - 1], col_recv.at[d - 1], (sec, r, to))
-
-    def ws_copy(d):
-        to = lax.rem(me + d, N)
-        return copy(wire.at[to], wgot.at[d - 1], ws_send.at[d - 1], ws_recv.at[d - 1], peer(to))
+        return copy(gath.at[slot], gath.at[slot], row_send.at[d - 1], row_recv.at[d - 1], row_peer(d))
+
+    def col_copy(d):
+        return copy(part.at[d - 1], got.at[d - 1], col_send.at[d - 1], col_recv.at[d - 1], col_peer(d))
+
+    def hand_copy():
+        return copy(feat, inc, hand_send, hand_recv, across)
+
+    def wx_copy(d):
+        to = lax.rem(r + d, R)
+        return copy(wire.at[to], xgot.at[d - 1], wx_send.at[d - 1], wx_recv.at[d - 1], row_peer(d))
+
+    def wz_copy(d, slot):
+        return copy(along.at[slot], along.at[slot], wz_send.at[d - 1], wz_recv.at[d - 1], col_peer(d))
 
     def wg_copy(d, slot):
-        return copy(wfull.at[slot], wfull.at[slot], wg_send.at[d - 1], wg_recv.at[d - 1], peer(lax.rem(me + d, N)))
-
-    def hand_copy():
-        return copy(feat, inc, hand_send, hand_recv, (1 - sec, r, c))
+        return copy(summed.at[slot], summed.at[slot], wg_send.at[d - 1], wg_recv.at[d - 1], row_peer(d))
+
+    def own_rows():
+        masked = jnp.where(pre[...] > 0, inc[...], jnp.zeros((nodes, width), jnp.bfloat16))
+        inc[...] = masked
+        gath[r] = lax.dot_general(
+            masked, weight[...], (((1,), (1,)), ((), ())), preferred_element_type=jnp.float32
+        ).astype(jnp.bfloat16)
 
     @pl.when(sec == 1)
     def _():
         inc[...] = out_grad[...]
-
-    pl.semaphore_wait(barrier, N)
+        own_rows()
+
+    pl.semaphore_wait(barrier, len(peers))
 
     @pl.when(sec == 0)
     def _():
         hand_copy().wait_recv()
-
-    masked = jnp.where(pre[...] > 0, inc[...], jnp.zeros((nodes, width), jnp.bfloat16))
-    gath[r] = lax.dot_general(
-        masked, weight[...], (((1,), (1,)), ((), ())), preferred_element_type=jnp.float32
-    ).astype(jnp.bfloat16)
+        own_rows()
+
     for d in range(1, R):
         row_copy(d, r).start()
 
     wire[...] = lax.dot_general(
-        agg[...], masked, (((0,), (0,)), ((), ())), preferred_element_type=jnp.float32
+        agg[...], inc[...], (((0,), (0,)), ((), ())), preferred_element_type=jnp.float32
     ).astype(jnp.bfloat16).reshape(wire.shape)
-
-    def start_weight():
-        for d in range(1, N):
-            ws_copy(d).start()
-
-    def gather_weight():
-        total = wire[me].astype(jnp.float32)
-        for d in range(1, N):
-            ws_copy(d).wait_recv()
-            total = total + wgot[d - 1].astype(jnp.float32)
-        wfull[me] = (total * scale).astype(jnp.bfloat16)
-        for d in range(1, N):
-            wg_copy(d, me).start()
-
-    @pl.when(sec == 0)
-    def _():
-        start_weight()
+    for d in range(1, R):
+        wx_copy(d).start()
 
     for d in range(1, R):
         row_copy(d, lax.rem(r + R - d, R)).wait_recv()
@@ -127,35 +121,56 @@
 
     for d in range(1, C):
         part[d - 1] = term(lax.rem(c + d, C)).astype(jnp.bfloat16)
-        col_copy(d, c).start()
+        col_copy(d).start()
     total = term(c)
+
+    def weight_along():
+        here = wire[r].astype(jnp.float32)
+        for d in range(1, R):
+            wx_copy(d).wait_recv()
+            here = here + xgot[d - 1].astype(jnp.float32)
+        along[c] = here.astype(jnp.bfloat16)
+        for d in range(1, C):
+            wz_copy(d, c).start()
 
     @pl.when(sec == 0)
     def _():
-        gather_weight()
+        weight_along()
 
     for d in range(1, C):
-        col_copy(d, c).wait_recv()
+        col_copy(d).wait_recv()
         total = total + got[d - 1].astype(jnp.float32)
     feat[...] = total.astype(jnp.bfloat16)
 
     @pl.when(sec == 1)
     def _():
         hand_copy().start()
-        start_weight()
-        gather_weight()
+        weight_along()
         hand_copy().wait_send()
 
-    for d in range(1, N):
-        wg_copy(d, lax.rem(me + N - d, N)).wait_recv()
-    wsum[...] = wfull[...]
+    for d in range(1, C):
+        wz_copy(d, lax.rem(c + C - d, C)).wait_recv()
+    whole = along[0].astype(jnp.float32)
+    for k in range(1, C):
+        whole = whole + along[k].astype(jnp.float32)
+    summed[r] = (whole * scale).astype(jnp.bfloat16)
+    for d in range(1, R):
+        wg_copy(d, r).start()
+    for d in range(1, R):
+        wg_copy(d, lax.rem(r + R - d, R)).wait_recv()
+    wsum[...] = summed[...].reshape(wsum.shape)
     for d in range(1, R):
         row_copy(d, r).wait_send()
+        wx_copy(d).wait_send()
+        wg_copy(d, r).wait_send()
     for d in range(1, C):
-        col_copy(d, c).wait_send()
-    for d in range(1, N):
-        ws_copy(d).wait_send()
-        wg_copy(d, me).wait_send()
+        col_copy(d).wait_send()
+        wz_copy(d, c).wait_send()
+
+
+def finish_kernel(wsum, feat, weight_grad, feature_grads):
+    weight_grad[...] = wsum[...].astype(jnp.float32)
+    feature_grads[...] = feat[...]
 
 
 def fused(out_grad, pre_act, aggregated, weights, tiles, tile_index, live_count):
@@ -180,12 +195,12 @@
         ],
         name="dense_tile",
     )(tile_index[0, 0].T, live_count, tiles[0, 0])
-    chunk = width // N
+    share = width // R
     scale = 1.0 / math.sqrt(nodes * N)
     wsum, feat = pl.pallas_call(
         functools.partial(layers_kernel, R, C, scale),
         out_shape=(
-            jax.ShapeDtypeStruct((N, chunk, width), bf16),
+            jax.ShapeDtypeStruct((width, width), bf16),
             jax.ShapeDtypeStruct((nodes, width), bf16),
         ),
         in_specs=[vmem] * 5,
@@ -195,16 +210,27 @@
             pltpu.VMEM((R, nodes, width), bf16),
             pltpu.VMEM((C - 1, nodes, width), bf16),
             pltpu.VMEM((C - 1, nodes, width), bf16),
-            pltpu.VMEM((N, chunk, width), bf16),
-            pltpu.VMEM((N - 1, chunk, width), bf16),
-            pltpu.VMEM((N, chunk, width), bf16),
-            dma((R - 1,)), dma((R - 1,)), dma((C - 1,)), dma((C - 1,)),
-            dma((N - 1,)), dma((N - 1,)), dma((N - 1,)), dma((N - 1,)), dma, dma,
+            pltpu.VMEM((R, share, width), bf16),
+            pltpu.VMEM((R - 1, share, width), bf16),
+            pltpu.VMEM((C, share, width), bf16),
+            pltpu.VMEM((R, share, width), bf16),
+            dma((R - 1,)), dma((R - 1,)), dma((C - 1,)), dma((C - 1,)), dma, dma,
+            dma((R - 1,)), dma((R - 1,)), dma((C - 1,)), dma((C - 1,)), dma((R - 1,)), dma((R - 1,)),
         ],
         compiler_params=pltpu.CompilerParams(collective_id=0, has_side_effects=True),
         name="both_layers",
     )(out_grad, pre_act[0], aggregated[0], weights[0], dense)
-    return (wsum.astype(f32).reshape(1, width, width), feat[None])
+    weight_grad, feature_grads = pl.pallas_call(
+        finish_kernel,
+        out_shape=(
+            jax.ShapeDtypeStruct((width, width), f32),
+            jax.ShapeDtypeStruct((nodes, width), bf16),
+        ),
+        in_specs=[vmem] * 2,
+        out_specs=(vmem, vmem),
+        name="finish",
+    )(wsum, feat)
+    return (weight_grad[None], feature_grads[None])
 
 
 def from_behind(value, axis, steps):

time: 37.9 us -> 37.4 us (0.987)
  Pallas kernels: 33.3 us -> 36 us
  other arithmetic: 1.63 us -> 0 us
  local copies, waits for them, and re-layouts: 1.47 us -> 0 us
    pallas_call x0 -> x1, Pallas kernels: none -> 1.65 us  [fused(): pl.pallas_call(finish_kernel, out_shape=(jax.ShapeDtypeStruct((width, wid...]
    reshape x1 -> x0, other arithmetic: 1.63 us -> none  [fused(): return (wsum.astype(f32).reshape(1, width, width), feat[None])]
    unnamed x1 -> x0, local copies, waits for them, and re-layouts: 1.47 us -> none
    pallas_call x1, Pallas kernels: 30.2 us -> 31.3 us  [fused(): pl.pallas_call(functools.partial(layers_kernel, R, C, scale), out_shape=(...]
where the time goes in v2:
time: 37.4 us; the launch traced here: 37.3 us
  Pallas kernels  36 us (96%)
  between operations  1.29 us (3%)
    pallas_call x1, Pallas kernels, fused(): pl.pallas_call(functools.partial(layers_kernel, R, C, scale), out_shape=(...  31.3 us
    pallas_call x1, Pallas kernels, fused(): pl.pallas_call(functools.partial(dense_kernel, col_blocks), out_shape=jax...  3.08 us
    pallas_call x1, Pallas kernels, fused(): pl.pallas_call(finish_kernel, out_shape=(jax.ShapeDtypeStruct((width, wid...  1.65 us

profile of v2, /device:TPU:0, one launch (start us, length us, event | category | flops | bytes accessed | tf_op | source)
XLA Modules:
  0.0 37.3 jit_solution(4760012860902542162)
XLA Ops:
  1.3 3.1 %dense_tile.1.dense = bf16[512,512]{1,0:T(8,128)(2,1)} custom-call(s32[2,64]{1,0:T(2,128)} %bitcast.13, s32[1,1]{1,0:T(1,128)S(6)} %copy.9.count, bf16[64,128,128]{2,1,0:T(8,128)(2,1)} %bitcast.9), custom_call_target="tpu_custom_call" | custom-call | tf_op jit(solution)/shard_map/dense_tile/pallas_call | solution.py:186
  4.4 31.3 %both_layers.1 = (bf16[256,256]{1,0:T(8,128)(2,1)}, bf16[128,256]{1,0:T(8,128)(2,1)}) custom-call(bf16[128,256]{1,0:T(8,128)(2,1)} %out_grad.1, bf16[128,256]{1,0:T(8,128)(2,1)} %bitcast.11, bf16[128,256]{1,0:T(8,128)(2,1)} %bitcast.12, bf16[256,256]{1,0:T(8,128)(2,1)} %bitcast.10, bf16[512,512]{1,0:T(8,128)(2,1)} %dense_tile.1.dense), custom_call_target="tpu_custom_call" | custom-call | tf_op jit(solution)/shard_map/both_layers/pallas_call | solution.py:200
  35.7 1.7 %finish.1 = (f32[256,256]{1,0:T(8,128)}, bf16[128,256]{1,0:T(8,128)(2,1)}) custom-call(bf16[256,256]{1,0:T(8,128)(2,1)} %get-tuple-element.6.wsum, bf16[128,256]{1,0:T(8,128)(2,1)} %get-tuple-element.7.feat), custom_call_target="tpu_custom_call" | custom-call | tf_op jit(solution)/shard_map/finish/pallas_call | solution.py:223

commit v3 on v2

--- a/solution.py
+++ b/solution.py
@@ -39,13 +39,13 @@
 
 
 def layers_kernel(
-    R, C, scale, out_grad, pre, agg, weight, dense, wsum, feat,
-    inc, gath, part, got, wire, xgot, along, summed,
+    R, C, scale, out_grad, pre_act, aggregated, weights, dense_tile, wsum, feat,
+    pre, agg, weight, dense, in_sems, inc, gath, part, got, wire, xgot, along, summed,
     row_send, row_recv, col_send, col_recv, hand_send, hand_recv,
     wx_send, wx_recv, wz_send, wz_recv, wg_send, wg_recv,
 ):
     sec, r, c = (lax.axis_index(a) for a in ("section", "row", "col"))
-    nodes, width = out_grad.shape
+    nodes, width = inc.shape
 
     def row_peer(d):
         return (sec, lax.rem(r + d, R), c)
@@ -58,6 +58,21 @@
     peers = [row_peer(d) for d in range(1, R)] + [col_peer(d) for d in range(1, C)] + [across]
     for to in peers:
         pl.semaphore_signal(barrier, inc=1, device_id=to, device_id_type=MESH)
+
+    load_inc = pltpu.make_async_copy(out_grad, inc, in_sems.at[0])
+    load_pre = pltpu.make_async_copy(pre_act, pre, in_sems.at[1])
+    load_weight = pltpu.make_async_copy(weights, weight, in_sems.at[2])
+    load_agg = pltpu.make_async_copy(aggregated, agg, in_sems.at[3])
+    load_dense = pltpu.make_async_copy(dense_tile, dense, in_sems.at[4])
+
+    @pl.when(sec == 1)
+    def _():
+        load_inc.start()
+
+    load_pre.start()
+    load_weight.start()
+    load_agg.start()
+    load_dense.start()
 
     def copy(src, dst, send, recv, to):
         return pltpu.make_async_remote_copy(
@@ -90,9 +105,12 @@
             masked, weight[...], (((1,), (1,)), ((), ())), preferred_element_type=jnp.float32
         ).astype(jnp.bfloat16)
 
+    load_pre.wait()
+    load_weight.wait()
+
     @pl.when(sec == 1)
     def _():
-        inc[...] = out_grad[...]
+        load_inc.wait()
         own_rows()
 
     pl.semaphore_wait(barrier, len(peers))
@@ -105,6 +123,7 @@
     for d in range(1, R):
         row_copy(d, r).start()
 
+    load_agg.wait()
     wire[...] = lax.dot_general(
         agg[...], inc[...], (((0,), (0,)), ((), ())), preferred_element_type=jnp.float32
     ).astype(jnp.bfloat16).reshape(wire.shape)
@@ -113,16 +132,7 @@
 
     for d in range(1, R):
         row_copy(d, lax.rem(r + R - d, R)).wait_recv()
-    spread = gath[...].reshape(R * nodes, width)
-
-    def term(to):
-        rows = pl.ds(pl.multiple_of(to * nodes, nodes), nodes)
-        return jnp.dot(dense[rows, :], spread, preferred_element_type=jnp.float32)
-
-    for d in range(1, C):
-        part[d - 1] = term(lax.rem(c + d, C)).astype(jnp.bfloat16)
-        col_copy(d).start()
-    total = term(c)
+    load_dense.wait()
 
     def weight_along():
         here = wire[r].astype(jnp.float32)
@@ -133,9 +143,34 @@
         for d in range(1, C):
             wz_copy(d, c).start()
 
+    def weight_back():
+        for d in range(1, C):
+            wz_copy(d, lax.rem(c + C - d, C)).wait_recv()
+        whole = along[0].astype(jnp.float32)
+        for k in range(1, C):
+            whole = whole + along[k].astype(jnp.float32)
+        summed[r] = (whole * scale).astype(jnp.bfloat16)
+        for d in range(1, R):
+            wg_copy(d, r).start()
+
     @pl.when(sec == 0)
     def _():
         weight_along()
+
+    spread = gath[...].reshape(R * nodes, width)
+
+    def term(to):
+        rows = pl.ds(pl.multiple_of(to * nodes, nodes), nodes)
+        return jnp.dot(dense[rows, :], spread, preferred_element_type=jnp.float32)
+
+    for d in range(1, C):
+        part[d - 1] = term(lax.rem(c + d, C)).astype(jnp.bfloat16)
+        col_copy(d).start()
+    total = term(c)
+
+    @pl.when(sec == 0)
+    def _():
+        weight_back()
 
     for d in range(1, C):
         col_copy(d).wait_recv()
@@ -146,16 +181,9 @@
     def _():
         hand_copy().start()
         weight_along()
+        weight_back()
         hand_copy().wait_send()
 
-    for d in range(1, C):
-        wz_copy(d, lax.rem(c + C - d, C)).wait_recv()
-    whole = along[0].astype(jnp.float32)
-    for k in range(1, C):
-        whole = whole + along[k].astype(jnp.float32)
-    summed[r] = (whole * scale).astype(jnp.bfloat16)
-    for d in range(1, R):
-        wg_copy(d, r).start()
     for d in range(1, R):
         wg_copy(d, lax.rem(r + R - d, R)).wait_recv()
     wsum[...] = summed[...].reshape(wsum.shape)
@@ -203,9 +231,14 @@
             jax.ShapeDtypeStruct((width, width), bf16),
             jax.ShapeDtypeStruct((nodes, width), bf16),
         ),
-        in_specs=[vmem] * 5,
+        in_specs=[pl.BlockSpec(memory_space=pl.ANY)] * 5,
         out_specs=(vmem, vmem),
         scratch_shapes=[
+            pltpu.VMEM((nodes, width), bf16),
+            pltpu.VMEM((nodes, width), bf16),
+            pltpu.VMEM((width, width), bf16),
+            pltpu.VMEM((rows, cols), bf16),
+            dma((5,)),
             pltpu.VMEM((nodes, width), bf16),
             pltpu.VMEM((R, nodes, width), bf16),
             pltpu.VMEM((C - 1, nodes, width), bf16),

time: 37.4 us -> 34.8 us (0.930)
  Pallas kernels: 36 us -> 33.3 us
    pallas_call x1, Pallas kernels: 31.3 us -> 28.5 us  [fused(): pl.pallas_call(functools.partial(layers_kernel, R, C, scale), out_shape=(...]
where the time goes in v3:
time: 34.8 us; the launch traced here: 34.6 us
  Pallas kernels  33.3 us (96%)
  between operations  1.29 us (4%)
    pallas_call x1, Pallas kernels, fused(): pl.pallas_call(functools.partial(layers_kernel, R, C, scale), out_shape=(...  28.5 us
    pallas_call x1, Pallas kernels, fused(): pl.pallas_call(functools.partial(dense_kernel, col_blocks), out_shape=jax...  3.08 us
    pallas_call x1, Pallas kernels, fused(): pl.pallas_call(finish_kernel, out_shape=(jax.ShapeDtypeStruct((width, wid...  1.65 us

profile of v3, /device:TPU:0, one launch (start us, length us, event | category | flops | bytes accessed | tf_op | source)
XLA Modules:
  0.0 34.6 jit_solution(11693335152132920664)
XLA Ops:
  1.3 3.1 %dense_tile.1 = bf16[512,512]{1,0:T(8,128)(2,1)} custom-call(s32[2,64]{1,0:T(2,128)} %bitcast.13, s32[1,1]{1,0:T(1,128)S(6)} %copy.9.count, bf16[64,128,128]{2,1,0:T(8,128)(2,1)} %bitcast.9), custom_call_target="tpu_custom_call" | custom-call | tf_op jit(solution)/shard_map/dense_tile/pallas_call | solution.py:214
  4.4 28.5 %both_layers.1 = (bf16[256,256]{1,0:T(8,128)(2,1)}, bf16[128,256]{1,0:T(8,128)(2,1)}) custom-call(bf16[128,256]{1,0:T(8,128)(2,1)} %out_grad.1, bf16[128,256]{1,0:T(8,128)(2,1)} %bitcast.11, bf16[128,256]{1,0:T(8,128)(2,1)} %bitcast.12, bf16[256,256]{1,0:T(8,128)(2,1)} %bitcast.10, bf16[512,512]{1,0:T(8,128)(2,1)} %dense_tile.1), custom_call_target="tpu_custom_call" | custom-call | tf_op jit(solution)/shard_map/both_layers/pallas_call | solution.py:228
  32.9 1.7 %finish.1 = (f32[256,256]{1,0:T(8,128)}, bf16[128,256]{1,0:T(8,128)(2,1)}) custom-call(bf16[256,256]{1,0:T(8,128)(2,1)} %get-tuple-element.6.wsum, bf16[128,256]{1,0:T(8,128)(2,1)} %get-tuple-element.7.feat), custom_call_target="tpu_custom_call" | custom-call | tf_op jit(solution)/shard_map/finish/pallas_call | solution.py:256

commit v4 on v3

--- a/solution.py
+++ b/solution.py
@@ -79,11 +79,15 @@
             src_ref=src, dst_ref=dst, send_sem=send, recv_sem=recv, device_id=to, device_id_type=MESH
         )
 
-    def row_copy(d, slot):
-        return copy(gath.at[slot], gath.at[slot], row_send.at[d - 1], row_recv.at[d - 1], row_peer(d))
-
-    def col_copy(d):
-        return copy(part.at[d - 1], got.at[d - 1], col_send.at[d - 1], col_recv.at[d - 1], col_peer(d))
+    half = width // 2
+
+    def row_copy(h, d, slot):
+        k = h * (R - 1) + d - 1
+        return copy(gath.at[h, slot], gath.at[h, slot], row_send.at[k], row_recv.at[k], row_peer(d))
+
+    def col_copy(h, d):
+        k = h * (C - 1) + d - 1
+        return copy(part.at[k], got.at[k], col_send.at[k], col_recv.at[k], col_peer(d))
 
     def hand_copy():
         return copy(feat, inc, hand_send, hand_recv, across)
@@ -101,9 +105,11 @@
     def own_rows():
         masked = jnp.where(pre[...] > 0, inc[...], jnp.zeros((nodes, width), jnp.bfloat16))
         inc[...] = masked
-        gath[r] = lax.dot_general(
+        rows = lax.dot_general(
             masked, weight[...], (((1,), (1,)), ((), ())), preferred_element_type=jnp.float32
         ).astype(jnp.bfloat16)
+        gath[0, r] = rows[:, :half]
+        gath[1, r] = rows[:, half:]
 
     load_pre.wait()
     load_weight.wait()
@@ -120,8 +126,9 @@
         hand_copy().wait_recv()
         own_rows()
 
-    for d in range(1, R):
-        row_copy(d, r).start()
+    for h in range(2):
+        for d in range(1, R):
+            row_copy(h, d, r).start()
 
     load_agg.wait()
     wire[...] = lax.dot_general(
@@ -130,8 +137,6 @@
     for d in range(1, R):
         wx_copy(d).start()
 
-    for d in range(1, R):
-        row_copy(d, lax.rem(r + R - d, R)).wait_recv()
     load_dense.wait()
 
     def weight_along():
@@ -153,29 +158,35 @@
         for d in range(1, R):
             wg_copy(d, r).start()
 
+    totals = []
+    for h in range(2):
+        for d in range(1, R):
+            row_copy(h, d, lax.rem(r + R - d, R)).wait_recv()
+        if h == 1:
+            @pl.when(sec == 0)
+            def _():
+                weight_along()
+        spread = gath[h].reshape(R * nodes, half)
+
+        def term(to):
+            rows = pl.ds(pl.multiple_of(to * nodes, nodes), nodes)
+            return jnp.dot(dense[rows, :], spread, preferred_element_type=jnp.float32)
+
+        for d in range(1, C):
+            part[h * (C - 1) + d - 1] = term(lax.rem(c + d, C)).astype(jnp.bfloat16)
+            col_copy(h, d).start()
+        totals.append(term(c))
+
     @pl.when(sec == 0)
     def _():
-        weight_along()
-
-    spread = gath[...].reshape(R * nodes, width)
-
-    def term(to):
-        rows = pl.ds(pl.multiple_of(to * nodes, nodes), nodes)
-        return jnp.dot(dense[rows, :], spread, preferred_element_type=jnp.float32)
-
-    for d in range(1, C):
-        part[d - 1] = term(lax.rem(c + d, C)).astype(jnp.bfloat16)
-        col_copy(d).start()
-    total = term(c)
-
-    @pl.when(sec == 0)
-    def _():
         weight_back()
 
-    for d in range(1, C):
-        col_copy(d).wait_recv()
-        total = total + got[d - 1].astype(jnp.float32)
-    feat[...] = total.astype(jnp.bfloat16)
+    for h in range(2):
+        total = totals[h]
+        for d in range(1, C):
+            col_copy(h, d).wait_recv()
+            total = total + got[h * (C - 1) + d - 1].astype(jnp.float32)
+        feat[:, h * half:(h + 1) * half] = total.astype(jnp.bfloat16)
 
     @pl.when(sec == 1)
     def _():
@@ -188,11 +199,13 @@
         wg_copy(d, lax.rem(r + R - d, R)).wait_recv()
     wsum[...] = summed[...].reshape(wsum.shape)
     for d in range(1, R):
-        row_copy(d, r).wait_send()
+        for h in range(2):
+            row_copy(h, d, r).wait_send()
         wx_copy(d).wait_send()
         wg_copy(d, r).wait_send()
     for d in range(1, C):
-        col_copy(d).wait_send()
+        for h in range(2):
+            col_copy(h, d).wait_send()
         wz_copy(d, c).wait_send()
 
 
@@ -240,14 +253,14 @@
             pltpu.VMEM((rows, cols), bf16),
             dma((5,)),
             pltpu.VMEM((nodes, width), bf16),
-            pltpu.VMEM((R, nodes, width), bf16),
-            pltpu.VMEM((C - 1, nodes, width), bf16),
-            pltpu.VMEM((C - 1, nodes, width), bf16),
+            pltpu.VMEM((2, R, nodes, width // 2), bf16),
+            pltpu.VMEM((2 * (C - 1), nodes, width // 2), bf16),
+            pltpu.VMEM((2 * (C - 1), nodes, width // 2), bf16),
             pltpu.VMEM((R, share, width), bf16),
             pltpu.VMEM((R - 1, share, width), bf16),
             pltpu.VMEM((C, share, width), bf16),
             pltpu.VMEM((R, share, width), bf16),
-            dma((R - 1,)), dma((R - 1,)), dma((C - 1,)), dma((C - 1,)), dma, dma,
+            dma((2 * (R - 1),)), dma((2 * (R - 1),)), dma((2 * (C - 1),)), dma((2 * (C - 1),)), dma, dma,
             dma((R - 1,)), dma((R - 1,)), dma((C - 1,)), dma((C - 1,)), dma((R - 1,)), dma((R - 1,)),
         ],
         compiler_params=pltpu.CompilerParams(collective_id=0, has_side_effects=True),

time: 34.8 us -> 34.6 us (level)
    pallas_call x1, Pallas kernels: 28.5 us -> 28 us  [fused(): pl.pallas_call(functools.partial(layers_kernel, R, C, scale), out_shape=(...]
where the time goes in v4:
time: 34.6 us; the launch traced here: 34.4 us
  Pallas kernels  33.1 us (96%)
  between operations  1.29 us (4%)
    pallas_call x1, Pallas kernels, fused(): pl.pallas_call(functools.partial(layers_kernel, R, C, scale), out_shape=(...  28 us
    pallas_call x1, Pallas kernels, fused(): pl.pallas_call(functools.partial(dense_kernel, col_blocks), out_shape=jax...  3.42 us
    pallas_call x1, Pallas kernels, fused(): pl.pallas_call(finish_kernel, out_shape=(jax.ShapeDtypeStruct((width, wid...  1.65 us

profile of v4, /device:TPU:0, one launch (start us, length us, event | category | flops | bytes accessed | tf_op | source)
XLA Modules:
  0.0 34.4 jit_solution(10388030478477180519)
XLA Ops:
  1.3 3.4 %dense_tile.1 = bf16[512,512]{1,0:T(8,128)(2,1)} custom-call(s32[2,64]{1,0:T(2,128)} %bitcast.13, s32[1,1]{1,0:T(1,128)S(6)} %copy.9.count, bf16[64,128,128]{2,1,0:T(8,128)(2,1)} %bitcast.9), custom_call_target="tpu_custom_call" | custom-call | tf_op jit(solution)/shard_map/dense_tile/pallas_call | solution.py:227
  4.7 28.0 %both_layers.1 = (bf16[256,256]{1,0:T(8,128)(2,1)}, bf16[128,256]{1,0:T(8,128)(2,1)}) custom-call(bf16[128,256]{1,0:T(8,128)(2,1)} %out_grad.1, bf16[128,256]{1,0:T(8,128)(2,1)} %bitcast.11, bf16[128,256]{1,0:T(8,128)(2,1)} %bitcast.12, bf16[256,256]{1,0:T(8,128)(2,1)} %bitcast.10, bf16[512,512]{1,0:T(8,128)(2,1)} %dense_tile.1), custom_call_target="tpu_custom_call" | custom-call | tf_op jit(solution)/shard_map/both_layers/pallas_call | solution.py:241
  32.7 1.7 %finish.1 = (f32[256,256]{1,0:T(8,128)}, bf16[128,256]{1,0:T(8,128)(2,1)}) custom-call(bf16[256,256]{1,0:T(8,128)(2,1)} %get-tuple-element.6.wsum, bf16[128,256]{1,0:T(8,128)(2,1)} %get-tuple-element.7.feat), custom_call_target="tpu_custom_call" | custom-call | tf_op jit(solution)/shard_map/finish/pallas_call | solution.py:269
